TPU v7x, 32 devices: a whole 2x2x4 slice. The times are simulated.
32 devices in a mesh: groups: 2 (over y), obs: 4 (over z), hid: 2 (over x), rep: 2 (over core).
Axes of the slice: x: 2, y: 2, z: 4, core: 2. Of those that a mesh axis runs over, the one named last changes fastest.
Arguments:
- particles: float32 [8, 128, 512], P(('groups', 'obs')), parts along dimension 0, may hold values from -6 to 6
- obs_embed: bfloat16 [32768, 256], P(('groups', 'obs', 'rep')), parts along dimension 0, may hold values from -6 to 6
- step_index: int32 [2], P('groups'), parts along dimension 0, may hold values from 1 to 63
- noise: float32 [8, 128, 512], P('groups', 'obs'), parts along dimension 0, may hold values from -6 to 6
- w_query: bfloat16 [512, 2048], P(None, 'hid'), may hold values from -0.25 to 0.25
- w_key: bfloat16 [256, 2048], P(None, 'hid'), may hold values from -0.375 to 0.375
- w_value: bfloat16 [256, 2048], P(None, 'hid'), may hold values from -0.375 to 0.375
- w_time: bfloat16 [256, 16], P(None, 'hid'), may hold values from -0.375 to 0.375
- w_score: bfloat16 [2048, 512], P('hid'), may hold values from -0.0009765625 to 0.0009765625
- prior_in: bfloat16 [512, 2048], P(None, 'hid'), may hold values from -0.25 to 0.25
- prior_time: bfloat16 [256, 2048], P(None, 'hid'), may hold values from -0.375 to 0.375
- prior_out: bfloat16 [2048, 512], P('hid'), may hold values from -7.6293945e-06 to 7.6293945e-06
Outputs:
- updated: float32 [8, 128, 512], P('groups', 'obs'), parts along dimension 0
- score_total: float32 [8, 128, 512], P('groups', 'obs'), parts along dimension 0
There are 2 independent parts, one for each index of `groups`. A program takes and returns all parts, laid end to end along the dimension named above; an argument that names none is the same for every part. Nothing has to cross between parts.
All inputs are finite; a program needn't handle non-finite values.
Results may differ from a plain program's by a relative error of at most 0.0042.
Values may be sent and summed in bfloat16 or wider, within the bound.
No kernel may reach another device: no remote copies, remote signals or barrier semaphores. Data moves between devices by JAX's collectives and lax.ppermute only.
A program may use at most 64 MiB of HBM per device.

v0:
```python
import math
import jax
import jax.numpy as jnp
from jax import lax
from jax.sharding import PartitionSpec as P

DH = 128
STEPS = 64
SIG_LO = 0.05
SIG_HI = 1.0


def passed_along(shard, axis, by):
    size = lax.axis_size(axis)
    return lax.ppermute(shard, axis, [(i, (i + by) % size) for i in range(size)])


def plan(step_index, feature_count):
    level = step_index[0].astype(jnp.float32)
    growth = math.log(SIG_HI / SIG_LO) / (STEPS - 1)
    sigma_now = SIG_LO * jnp.exp(growth * level)
    sigma_prev = SIG_LO * jnp.exp(growth * (level - 1.0))
    delta = sigma_now * sigma_now - sigma_prev * sigma_prev
    halves = feature_count // 2
    frequency = jnp.exp(-math.log(1000.0) / halves * jnp.arange(halves).astype(jnp.float32))
    angles = 10.0 * jnp.log(sigma_now) * frequency
    features = jnp.concatenate([jnp.sin(angles), jnp.cos(angles)])[None, :].astype(jnp.bfloat16)
    return (features, delta)


def pair_pool(queries, keys, values, head_bias):
    count = queries.shape[0]
    query_heads = queries.reshape(count, -1, DH)
    key_heads = keys.reshape(keys.shape[0], -1, DH)
    value_heads = values.reshape(values.shape[0], -1, DH)
    scores = jnp.einsum("phd,jhd->phj", query_heads, key_heads, preferred_element_type=jnp.float32)
    weights = jax.nn.silu(scores * (1.0 / math.sqrt(DH)) + head_bias[None, :, None]).astype(
        jnp.bfloat16
    )
    pooled = jnp.einsum("phj,jhd->phd", weights, value_heads, preferred_element_type=jnp.float32)
    return pooled.reshape(count, -1)


def on_device(
    particles,
    obs_embed,
    step_index,
    noise,
    w_query,
    w_key,
    w_value,
    w_time,
    w_score,
    prior_in,
    prior_time,
    prior_out,
):
    obs_count = lax.axis_size("obs")
    rep_count = lax.axis_size("rep")
    features, delta = plan(step_index, w_time.shape[0])
    head_bias = jnp.dot(features, w_time, preferred_element_type=jnp.float32)[0]
    keys = jnp.dot(obs_embed, w_key, preferred_element_type=jnp.float32).astype(jnp.bfloat16)
    values = jnp.dot(obs_embed, w_value, preferred_element_type=jnp.float32).astype(jnp.bfloat16)
    home = particles[0]
    block_rows = home.shape[0]
    width = home.shape[1]
    stripe = block_rows // obs_count
    owned = home.reshape(obs_count, stripe, width)
    theta_owner = lax.all_to_all(owned, "obs", split_axis=0, concat_axis=0, tiled=True)
    moving = home.astype(jnp.bfloat16)

    def pool(travel):
        queries = jnp.dot(travel, w_query, preferred_element_type=jnp.float32).astype(jnp.bfloat16)
        return pair_pool(queries, keys, values, head_bias)

    score_weight = w_score.astype(jnp.float32)

    def turn(turn_index, cycle_state):
        arrived = passed_along(cycle_state[0], "obs", 1)
        totals = passed_along(cycle_state[1], "obs", 1)
        return (arrived, totals + pool(arrived))

    cycle_state = lax.fori_loop(0, obs_count - 1, turn, (moving, pool(moving)))
    pieces = cycle_state[1].reshape(obs_count, stripe, -1)
    flat = pieces.reshape(-1, pieces.shape[-1])
    result = jnp.dot(
        flat, score_weight, precision=lax.Precision.HIGHEST, preferred_element_type=jnp.float32
    )
    pieces = result.reshape(pieces.shape[:-1] + (width,))
    received = lax.all_to_all(pieces, "obs", split_axis=0, concat_axis=0, tiled=True)
    summed = jnp.roll(received, 1, axis=0)
    owner_rows = theta_owner.reshape(block_rows, width)
    share = block_rows // rep_count
    start = lax.axis_index("rep") * share
    my_rows = lax.dynamic_slice_in_dim(owner_rows, start, share, 0).astype(jnp.bfloat16)
    prior_pre = jnp.dot(my_rows, prior_in, preferred_element_type=jnp.float32) + jnp.dot(
        features, prior_time, preferred_element_type=jnp.float32
    )
    prior_hidden = jax.nn.silu(prior_pre).astype(jnp.bfloat16)
    prior_part = jnp.dot(prior_hidden, prior_out, preferred_element_type=jnp.float32)
    total_count = obs_embed.shape[0] * obs_count * rep_count
    scores_flat = summed.reshape(block_rows, width)
    current = lax.dynamic_slice_in_dim(scores_flat, start, share, 0)
    scores_flat = lax.dynamic_update_slice_in_dim(
        scores_flat, current - (total_count - 1) * prior_part, start, 0
    )
    score_total = lax.psum(scores_flat, ("hid", "rep")).reshape(obs_count, stripe, width)
    updated = theta_owner + delta * score_total + jnp.sqrt(delta) * noise
    return (updated, score_total)


def solution(mesh):
    in_specs = (
        P(("groups", "obs"), None, None),
        P(("groups", "obs", "rep"), None),
        P("groups"),
        P("groups", "obs", None),
        P(None, "hid"),
        P(None, "hid"),
        P(None, "hid"),
        P(None, "hid"),
        P("hid", None),
        P(None, "hid"),
        P(None, "hid"),
        P("hid", None),
    )
    out_specs = (P("groups", "obs", None), P("groups", "obs", None))
    return jax.shard_map(
        on_device, mesh=mesh, in_specs=in_specs, out_specs=out_specs, check_vma=False
    )
```

profile of v0, /device:TPU:0, one launch (start us, length us, event | category | flops | bytes accessed | tf_op | source)
XLA Modules:
  0.0 154.7 jit_solution(1549332694135412617)
XLA Ops:
  8.4 4.3 %convolution_convert_fusion.2 = bf16[2048,1024]{0,1:T(8,128)(2,1)} fusion(bf16[2048,256]{1,0:T(8,128)(2,1)S(1)} %copy-done, bf16[256,1024]{1,0:T(8,128)(2,1)} %param.20), kind=kOutput, calls=%fused_computation.23 | convolution fusion | flops 1075838976 | bytes 5767168 | tf_op jit(solution)/shard_map/dot_general | solution.py:63
  12.8 3.3 %convolution_convert_fusion.1 = bf16[2048,1024]{0,1:T(8,128)(2,1)} fusion(bf16[2048,256]{1,0:T(8,128)(2,1)S(1)} %copy-done, bf16[256,1024]{1,0:T(8,128)(2,1)S(1)} %copy-done.4), kind=kOutput, calls=%fused_computation.22 | convolution fusion | flops 1075838976 | bytes 5767168 | tf_op jit(solution)/shard_map/dot_general | solution.py:62
  16.1 6.5 %copy.19 = bf16[2048,1024]{1,0:T(8,128)(2,1)} copy(bf16[2048,1024]{0,1:T(8,128)(2,1)} %convolution_convert_fusion.1) | data formatting | bytes 8388608 | tf_op jit(solution)/shard_map/while | solution.py:83
  23.0 8.8 %fusion.20 = f32[8,128,128]{2,1,0:T(8,128)} fusion(bf16[2048,8,128]{0,2,1:T(8,128)(2,1)} %bitcast.116, bf16[2048,8,128]{0,2,1:T(8,128)(2,1)} %bitcast.115, f32[8]{0:T(128)S(1)} %bitcast.124, bf16[16,8,8,128]{3,2,1,0:T(8,128)(2,1)S(1)} %fusion.21), kind=kOutput, calls=%fused_computation.24 | convolution fusion | flops 1088421888 | bytes 9175072 | tf_op jit(solution)/shard_map/phj,jhd->phd/dot_general | solution.py:40
  31.9 56.9 %while.12 = (s32[]{:T(128)}, bf16[128,512]{1,0:T(8,128)(2,1)S(1)}, f32[128,1024]{0,1:T(8,128)}, bf16[512,1024]{1,0:T(8,128)(2,1)S(1)}, bf16[2048,1024]{1,0:T(8,1...) while((s32[]{:T(128)}, bf16[128,512]{1,0:T(8,128)(2,1)S(1)}, ...), condition=%wide.region_1.2_spmd, body=%wide.region_0.1_spmd.sunk | while | flops 1222901760 | bytes 15073477 | solution.py:83
  31.9 3.0 %collective-permute-start = (bf16[128,512]{1,0:T(8,128)(2,1)S(1)}, bf16[128,512]{1,0:T(8,128)(2,1)S(1)}, u32[]{:S(2)}, u32[]{:S(2)}) collective-permute-start(bf16[128,512]{1,0:T(8,128)(2,1)S(1)} %get-tuple-element.115), channel_id=1, source_target_pairs={{0,4},{4,8},{8,12},{12,0},{1,5},{5,9},{9,13},{13,1},{2,6},{6,10},{... | collective-permute-start | bytes 393224 | tf_op jit(solution)/shard_map/while/body/eval_jaxpr/ppermute | solution.py:15
  34.9 1.6 %collective-permute-start.1 = (f32[128,1024]{0,1:T(8,128)}, f32[128,1024]{0,1:T(8,128)S(1)}, u32[]{:S(2)}, u32[]{:S(2)}) collective-permute-start(f32[128,1024]{0,1:T(8,128)} %get-tuple-element.116), channel_id=1, source_target_pairs={{0,4},{4,8},{8,12},{12,0},{1,5},{5,9},{9,13},{13,1},{2,6},{6,10},{... | collective-permute-start | bytes 1572872 | tf_op jit(solution)/shard_map/while/body/eval_jaxpr/ppermute | solution.py:15
  36.5 4.8 %collective-permute-done = bf16[128,512]{1,0:T(8,128)(2,1)S(1)} collective-permute-done((bf16[128,512]{1,0:T(8,128)(2,1)S(1)}, bf16[128,512]{1,0:T(8,128)(2,1)S(1)}, u32[]{:S(2)}, u32[]{:S(2)}) %collective-permute-start) | collective-permute-done | bytes 131104 | tf_op jit(solution)/shard_map/while/body/eval_jaxpr/ppermute | solution.py:15
  41.6 6.3 %fusion.73 = f32[8,128,128]{1,2,0:T(8,128)S(1)} fusion(bf16[2048,8,128]{0,2,1:T(8,128)(2,1)} %bitcast.117, f32[8]{0:T(128)S(1)} %bitcast.125, bf16[16,8,8,128]{3,2,1,0:T(8,128)(2,1)S(1)} %fusion.72, bf16[2048,1024]{1,0:T(8,128)(2,1)} %get-tuple-element.126), kind=kOutput, calls=%fused_computation.8.clone.1 | convolution fusion | flops 1088421888 | bytes 9175072 | tf_op jit(solution)/shard_map/while/body/eval_jaxpr/phj,jhd->phd/dot_general | solution.py:40
  47.9 3.8 %collective-permute-done.1 = f32[128,1024]{0,1:T(8,128)S(1)} collective-permute-done((f32[128,1024]{0,1:T(8,128)}, f32[128,1024]{0,1:T(8,128)S(1)}, u32[]{:S(2)}, u32[]{:S(2)}) %collective-permute-start.1) | collective-permute-done | bytes 524320 | tf_op jit(solution)/shard_map/while/body/eval_jaxpr/ppermute | solution.py:15
  53.8 6.9 %collective-permute-done = bf16[128,512]{1,0:T(8,128)(2,1)S(1)} collective-permute-done((bf16[128,512]{1,0:T(8,128)(2,1)S(1)}, bf16[128,512]{1,0:T(8,128)(2,1)S(1)}, u32[]{:S(2)}, u32[]{:S(2)}) %collective-permute-start) | collective-permute-done | bytes 131104 | tf_op jit(solution)/shard_map/while/body/eval_jaxpr/ppermute | solution.py:15
  61.1 6.3 %fusion.73 = f32[8,128,128]{1,2,0:T(8,128)S(1)} fusion(bf16[2048,8,128]{0,2,1:T(8,128)(2,1)} %bitcast.117, f32[8]{0:T(128)S(1)} %bitcast.125, bf16[16,8,8,128]{3,2,1,0:T(8,128)(2,1)S(1)} %fusion.72, bf16[2048,1024]{1,0:T(8,128)(2,1)} %get-tuple-element.126), kind=kOutput, calls=%fused_computation.8.clone.1 | convolution fusion | flops 1088421888 | bytes 9175072 | tf_op jit(solution)/shard_map/while/body/eval_jaxpr/phj,jhd->phd/dot_general | solution.py:40
  67.4 2.9 %collective-permute-done.1 = f32[128,1024]{0,1:T(8,128)S(1)} collective-permute-done((f32[128,1024]{0,1:T(8,128)}, f32[128,1024]{0,1:T(8,128)S(1)}, u32[]{:S(2)}, u32[]{:S(2)}) %collective-permute-start.1) | collective-permute-done | bytes 524320 | tf_op jit(solution)/shard_map/while/body/eval_jaxpr/ppermute | solution.py:15
  71.1 8.2 %collective-permute-done = bf16[128,512]{1,0:T(8,128)(2,1)S(1)} collective-permute-done((bf16[128,512]{1,0:T(8,128)(2,1)S(1)}, bf16[128,512]{1,0:T(8,128)(2,1)S(1)}, u32[]{:S(2)}, u32[]{:S(2)}) %collective-permute-start) | collective-permute-done | bytes 131104 | tf_op jit(solution)/shard_map/while/body/eval_jaxpr/ppermute | solution.py:15
  79.7 6.3 %fusion.73 = f32[8,128,128]{1,2,0:T(8,128)S(1)} fusion(bf16[2048,8,128]{0,2,1:T(8,128)(2,1)} %bitcast.117, f32[8]{0:T(128)S(1)} %bitcast.125, bf16[16,8,8,128]{3,2,1,0:T(8,128)(2,1)S(1)} %fusion.72, bf16[2048,1024]{1,0:T(8,128)(2,1)} %get-tuple-element.126), kind=kOutput, calls=%fused_computation.8.clone.1 | convolution fusion | flops 1088421888 | bytes 9175072 | tf_op jit(solution)/shard_map/while/body/eval_jaxpr/phj,jhd->phd/dot_general | solution.py:40
  86.0 2.0 %collective-permute-done.1 = f32[128,1024]{0,1:T(8,128)S(1)} collective-permute-done((f32[128,1024]{0,1:T(8,128)}, f32[128,1024]{0,1:T(8,128)S(1)}, u32[]{:S(2)}, u32[]{:S(2)}) %collective-permute-start.1) | collective-permute-done | bytes 524320 | tf_op jit(solution)/shard_map/while/body/eval_jaxpr/ppermute | solution.py:15
  88.8 2.2 %fusion.36 = f32[128,512]{1,0:T(8,128)S(1)} fusion(f32[128,1024]{0,1:T(8,128)} %get-tuple-element.39, bf16[1024,512]{1,0:T(8,128)(2,1)} %param.22), kind=kOutput, calls=%fused_computation.49 | convolution fusion | flops 805306368 | bytes 1835008 | tf_op jit(solution)/shard_map/dot_general | solution.py:86
  91.0 9.5 %all_to_all.10 = f32[4,32,512]{2,1,0:T(8,128)S(1)} all-to-all(f32[4,32,512]{2,1,0:T(8,128)S(1)} %bitcast.119), channel_id=1, replica_groups=mesh['groups'=2,'obs'=4,'hid'=2,'rep'=2] {'obs'}, dimensions={0} | all-to-all | bytes 524288 | tf_op jit(solution)/shard_map/all_to_all | solution.py:90
  100.5 3.4 %all-to-all-start = ((f32[4,32,512]{2,1,0:T(8,128)}), f32[4,32,512]{2,1,0:T(8,128)S(1)}, u32[]{:S(2)}, u32[]{:S(2)}) async-start(f32[4,32,512]{2,1,0:T(8,128)} %bitcast.120), calls=%async_computation | async-start | bytes 524288 | tf_op jit(solution)/shard_map/all_to_all | solution.py:69
  105.2 5.4 %all-to-all-done = f32[4,32,512]{2,1,0:T(8,128)S(1)} async-done(((f32[4,32,512]{2,1,0:T(8,128)}), f32[4,32,512]{2,1,0:T(8,128)S(1)}, u32[]{:S(2)}, u32[]{:S(2)}) %all-to-all-start) | async-done | bytes 262176 | tf_op jit(solution)/shard_map/all_to_all | solution.py:69
  110.6 1.7 %fusion.23 = f32[128,512]{1,0:T(8,128)S(1)} fusion(f32[128,512]{1,0:T(8,128)S(1)} %bitcast.121, s32[]{:T(128)S(6)} %select_n.2, bf16[1024,512]{1,0:T(8,128)(2,1)S(1)} %copy-done.6, bf16[512,1024]{1,0:T(8,128)(2,1)} %param.23, f32[1024]{0:T(1024)S(1)} %bitcast.123, f32[128,512]{1,0:T(8,128)S(1)} %bitcast.118), kind=kOutput, calls=%fused_computation.30 | convolution fusion | flops 134676480 | bytes 2429952 | tf_op jit(solution)/shard_map/dot_general | solution.py:100
  113.2 31.3 %all-reduce.2.cloned.1.call-done = f32[4,32,512]{2,1,0:T(8,128)} async-done(((f32[4,32,512]{2,1,0:T(8,128)}), f32[4,32,512]{2,1,0:T(8,128)}) %all-reduce.2.cloned.1.call-update) | async-done | bytes 262160 | tf_op jit(solution)/shard_map/psum | solution.py:107
  144.5 1.7 %multiply_add_fusion = f32[4,32,512]{2,1,0:T(8,128)} fusion(f32[4,32,512]{2,1,0:T(8,128)S(1)} %copy-done.5, f32[4,32,512]{2,1,0:T(8,128)S(1)} %all-to-all-done, f32[4,32,512]{2,1,0:T(8,128)} %all-reduce.2.cloned.1.call-done, f32[]{:T(128)S(6)} %sqrt.3, f32[]{:T(128)} %bitcast.6), kind=kLoop, calls=%fused_computation.34 | loop fusion | flops 262144 | bytes 1048584 | tf_op jit(solution)/shard_map/add | solution.py:108
  146.2 1.7 %copy.57 = f32[4,32,512]{2,1,0:T(8,128)} copy(f32[4,32,512]{2,1,0:T(8,128)} %all-reduce.2.cloned.1.call-done) | data formatting | bytes 524288
  (41 shorter events, 7.8 us)
Async XLA Ops:
  7.2 1.2 copy-start
  8.4 4.4 %copy-start.4 = (bf16[256,1024]{1,0:T(8,128)(2,1)S(1)}, bf16[256,1024]{1,0:T(8,128)(2,1)}, u32[]{:S(2)}) copy-start(bf16[256,1024]{1,0:T(8,128)(2,1)} %param.19) | copy-start | bytes 1572868
  12.8 3.3 %copy-start.2 = (f32[1,128,512]{2,1,0:T(8,128)S(1)}, f32[1,128,512]{2,1,0:T(8,128)}, u32[]{:S(2)}) copy-start(f32[1,128,512]{2,1,0:T(8,128)} %param.14) | copy-start | bytes 786436
  16.1 6.5 %copy-start.7 = (bf16[256,8]{0,1:T(8,128)(2,1)S(1)}, bf16[256,8]{0,1:T(8,128)(2,1)}, u32[]{:S(2)}) copy-start(bf16[256,8]{0,1:T(8,128)(2,1)} %param.21) | copy-start | bytes 12292
  16.1 6.6 %copy-start.1 = (bf16[512,1024]{1,0:T(8,128)(2,1)S(1)}, bf16[512,1024]{1,0:T(8,128)(2,1)}, u32[]{:S(2)}) copy-start(bf16[512,1024]{1,0:T(8,128)(2,1)} %param.18) | copy-start | bytes 3145732
  31.9 9.4 %collective-permute-start = (bf16[128,512]{1,0:T(8,128)(2,1)S(1)}, bf16[128,512]{1,0:T(8,128)(2,1)S(1)}, u32[]{:S(2)}, u32[]{:S(2)}) collective-permute-start(bf16[128,512]{1,0:T(8,128)(2,1)S(1)} %get-tuple-element.115), channel_id=1, source_target_pairs={{0,4},{4,8},{8,12},{12,0},{1,5},{5,9},{9,13},{13,1},{2,6},{6,10},{... | collective-permute-start | bytes 393224 | tf_op jit(solution)/shard_map/while/body/eval_jaxpr/ppermute | solution.py:15
  34.9 16.7 %collective-permute-start.1 = (f32[128,1024]{0,1:T(8,128)}, f32[128,1024]{0,1:T(8,128)S(1)}, u32[]{:S(2)}, u32[]{:S(2)}) collective-permute-start(f32[128,1024]{0,1:T(8,128)} %get-tuple-element.116), channel_id=1, source_target_pairs={{0,4},{4,8},{8,12},{12,0},{1,5},{5,9},{9,13},{13,1},{2,6},{6,10},{... | collective-permute-start | bytes 1572872 | tf_op jit(solution)/shard_map/while/body/eval_jaxpr/ppermute | solution.py:15
  52.5 8.2 %collective-permute-start = (bf16[128,512]{1,0:T(8,128)(2,1)S(1)}, bf16[128,512]{1,0:T(8,128)(2,1)S(1)}, u32[]{:S(2)}, u32[]{:S(2)}) collective-permute-start(bf16[128,512]{1,0:T(8,128)(2,1)S(1)} %get-tuple-element.115), channel_id=1, source_target_pairs={{0,4},{4,8},{8,12},{12,0},{1,5},{5,9},{9,13},{13,1},{2,6},{6,10},{... | collective-permute-start | bytes 393224 | tf_op jit(solution)/shard_map/while/body/eval_jaxpr/ppermute | solution.py:15
  52.5 17.7 %collective-permute-start.1 = (f32[128,1024]{0,1:T(8,128)}, f32[128,1024]{0,1:T(8,128)S(1)}, u32[]{:S(2)}, u32[]{:S(2)}) collective-permute-start(f32[128,1024]{0,1:T(8,128)} %get-tuple-element.116), channel_id=1, source_target_pairs={{0,4},{4,8},{8,12},{12,0},{1,5},{5,9},{9,13},{13,1},{2,6},{6,10},{... | collective-permute-start | bytes 1572872 | tf_op jit(solution)/shard_map/while/body/eval_jaxpr/ppermute | solution.py:15
  71.1 8.2 %collective-permute-start = (bf16[128,512]{1,0:T(8,128)(2,1)S(1)}, bf16[128,512]{1,0:T(8,128)(2,1)S(1)}, u32[]{:S(2)}, u32[]{:S(2)}) collective-permute-start(bf16[128,512]{1,0:T(8,128)(2,1)S(1)} %get-tuple-element.115), channel_id=1, source_target_pairs={{0,4},{4,8},{8,12},{12,0},{1,5},{5,9},{9,13},{13,1},{2,6},{6,10},{... | collective-permute-start | bytes 393224 | tf_op jit(solution)/shard_map/while/body/eval_jaxpr/ppermute | solution.py:15
  71.1 16.8 %collective-permute-start.1 = (f32[128,1024]{0,1:T(8,128)}, f32[128,1024]{0,1:T(8,128)S(1)}, u32[]{:S(2)}, u32[]{:S(2)}) collective-permute-start(f32[128,1024]{0,1:T(8,128)} %get-tuple-element.116), channel_id=1, source_target_pairs={{0,4},{4,8},{8,12},{12,0},{1,5},{5,9},{9,13},{13,1},{2,6},{6,10},{... | collective-permute-start | bytes 1572872 | tf_op jit(solution)/shard_map/while/body/eval_jaxpr/ppermute | solution.py:15
  88.8 21.9 %copy-start.6 = (bf16[1024,512]{1,0:T(8,128)(2,1)S(1)}, bf16[1024,512]{1,0:T(8,128)(2,1)}, u32[]{:S(2)}) copy-start(bf16[1024,512]{1,0:T(8,128)(2,1)} %param.25) | copy-start | bytes 3145732
  88.8 55.7 %copy-start.5 = (f32[4,32,512]{2,1,0:T(8,128)S(1)}, f32[4,32,512]{2,1,0:T(8,128)}, u32[]{:S(2)}) copy-start(f32[4,32,512]{2,1,0:T(8,128)} %param.17) | copy-start | bytes 786436
  100.5 10.2 %all-to-all-start = ((f32[4,32,512]{2,1,0:T(8,128)}), f32[4,32,512]{2,1,0:T(8,128)S(1)}, u32[]{:S(2)}, u32[]{:S(2)}) async-start(f32[4,32,512]{2,1,0:T(8,128)} %bitcast.120), calls=%async_computation | async-start | bytes 524288 | tf_op jit(solution)/shard_map/all_to_all | solution.py:69
  103.9 40.6 %all-reduce.2.cloned.1.call-start = ((), (), s32[]{:S(2)}) async-start(), calls=%async_computation.2 | async-start | bytes 524288 | tf_op jit(solution)/shard_map/psum | solution.py:107
  112.4 0.7 copy-start.3
Sparse Core Ops, SparseCore 0:
  113.2 31.2 all-reduce.1
where the time goes:
time: 155 us
  waiting for transfers between devices  65.3 us (42%)
  matrix products  41.7 us (27%)
  between operations  15.1 us (10%)
  blocking collectives  9.51 us (6%)
  starting transfers between devices  9.34 us (6%)
  local copies, waits for them, and re-layouts  9.31 us (6%)
  other arithmetic  4.42 us (3%)
    psum x1, waiting for transfers between devices, on_device(): lax.psum(scores_flat, ('hid', 'rep')).reshape(obs_count, stripe, width)  31.3 us
    ppermute x6, waiting for transfers between devices, passed_along(): lax.ppermute(shard, axis, [(i, (i + by) % size) for i in range(size)])  28.5 us
    dot_general x4, matrix products, pair_pool(): jnp.einsum('phj,jhd->phd', weights, value_heads, preferred_element_type=j...  27.6 us
    all_to_all x1, blocking collectives, on_device(): lax.all_to_all(pieces, 'obs', split_axis=0, concat_axis=0, tiled=True)  9.51 us
    while x1, local copies, waits for them, and re-layouts, on_device(): cycle_state = lax.fori_loop(0, obs_count - 1, turn, (moving, pool(moving)))  6.51 us
    ppermute x6, starting transfers between devices, passed_along(): lax.ppermute(shard, axis, [(i, (i + by) % size) for i in range(size)])  5.89 us
    all_to_all x1, waiting for transfers between devices, on_device(): lax.all_to_all(owned, 'obs', split_axis=0, concat_axis=0, tiled=True)  5.4 us
    dot_general x1, matrix products, on_device(): jnp.dot(obs_embed, w_value, preferred_element_type=jnp.float32)  4.35 us
  transfers between devices with their start and end apart: 8, of which 8 were waited for; matrix products, arithmetic and copies ran while one was open for 14% of the time, Pallas kernels for 0%

commit v1 on v0

--- a/solution.py
+++ b/solution.py
@@ -104,7 +104,9 @@
     scores_flat = lax.dynamic_update_slice_in_dim(
         scores_flat, current - (total_count - 1) * prior_part, start, 0
     )
-    score_total = lax.psum(scores_flat, ("hid", "rep")).reshape(obs_count, stripe, width)
+    score_total = jnp.sum(lax.all_gather(scores_flat, ("hid", "rep")), axis=0).reshape(
+        obs_count, stripe, width
+    )
     updated = theta_owner + delta * score_total + jnp.sqrt(delta) * noise
     return (updated, score_total)
 

time: 155 us -> 139 us (0.90)
  waiting for transfers between devices: 65.3 us -> 50 us
  local copies, waits for them, and re-layouts: 9.31 us -> 7.66 us
    psum x1 -> x0, waiting for transfers between devices: 31.3 us -> none  [on_device(): lax.psum(scores_flat, ('hid', 'rep')).reshape(obs_count, stripe, width)]
    all_gather x0 -> x1, waiting for transfers between devices: none -> 16.1 us  [on_device(): lax.all_gather(scores_flat, ('hid', 'rep'))]
    unnamed x17 -> x19, local copies, waits for them, and re-layouts: 2.74 us -> 1.09 us
  transfers between devices with their start and end apart: 8 -> 8, of which waited for: 8 -> 8; matrix products, arithmetic and copies ran while one was open for 14% -> 15% of each run, Pallas kernels for 0% -> 0%
where the time goes in v1:
time: 139 us; the launch traced here: 138 us
  waiting for transfers between devices  50 us (36%)
  matrix products  41.8 us (30%)
  between operations  15.1 us (11%)
  blocking collectives  9.65 us (7%)
  starting transfers between devices  9.34 us (7%)
  local copies, waits for them, and re-layouts  7.66 us (6%)
  other arithmetic  4.84 us (3%)
    ppermute x6, waiting for transfers between devices, passed_along(): lax.ppermute(shard, axis, [(i, (i + by) % size) for i in range(size)])  28.5 us
    dot_general x4, matrix products, pair_pool(): jnp.einsum('phj,jhd->phd', weights, value_heads, preferred_element_type=j...  27.7 us
    all_gather x1, waiting for transfers between devices, on_device(): lax.all_gather(scores_flat, ('hid', 'rep'))  16.1 us
    all_to_all x1, blocking collectives, on_device(): lax.all_to_all(pieces, 'obs', split_axis=0, concat_axis=0, tiled=True)  9.65 us
    while x1, local copies, waits for them, and re-layouts, on_device(): cycle_state = lax.fori_loop(0, obs_count - 1, turn, (moving, pool(moving)))  6.51 us
    ppermute x6, starting transfers between devices, passed_along(): lax.ppermute(shard, axis, [(i, (i + by) % size) for i in range(size)])  5.89 us
    all_to_all x1, waiting for transfers between devices, on_device(): lax.all_to_all(owned, 'obs', split_axis=0, concat_axis=0, tiled=True)  5.37 us
    dot_general x1, matrix products, on_device(): jnp.dot(obs_embed, w_value, preferred_element_type=jnp.float32)  4.36 us
  transfers between devices with their start and end apart: 8, of which 8 were waited for; matrix products, arithmetic and copies ran while one was open for 15% of the time, Pallas kernels for 0%

profile of v1, /device:TPU:0, one launch (start us, length us, event | category | flops | bytes accessed | tf_op | source)
XLA Modules:
  0.0 138.4 jit_solution(13304637071774757218)
XLA Ops:
  8.4 4.4 %convolution_convert_fusion.2 = bf16[2048,1024]{0,1:T(8,128)(2,1)} fusion(bf16[2048,256]{1,0:T(8,128)(2,1)S(1)} %copy-done, bf16[256,1024]{1,0:T(8,128)(2,1)} %param.20), kind=kOutput, calls=%fused_computation.23 | convolution fusion | flops 1075838976 | bytes 5767168 | tf_op jit(solution)/shard_map/dot_general | solution.py:63
  12.8 3.3 %convolution_convert_fusion.1 = bf16[2048,1024]{0,1:T(8,128)(2,1)} fusion(bf16[2048,256]{1,0:T(8,128)(2,1)S(1)} %copy-done, bf16[256,1024]{1,0:T(8,128)(2,1)S(1)} %copy-done.5), kind=kOutput, calls=%fused_computation.22 | convolution fusion | flops 1075838976 | bytes 5767168 | tf_op jit(solution)/shard_map/dot_general | solution.py:62
  16.1 6.5 %copy.25 = bf16[2048,1024]{1,0:T(8,128)(2,1)} copy(bf16[2048,1024]{0,1:T(8,128)(2,1)} %convolution_convert_fusion.1) | data formatting | bytes 8388608 | tf_op jit(solution)/shard_map/while | solution.py:83
  23.0 8.9 %fusion.20 = f32[8,128,128]{2,1,0:T(8,128)} fusion(bf16[2048,8,128]{0,2,1:T(8,128)(2,1)} %bitcast.121, bf16[2048,8,128]{0,2,1:T(8,128)(2,1)} %bitcast.120, f32[8]{0:T(128)S(1)} %bitcast.131, bf16[16,8,8,128]{3,2,1,0:T(8,128)(2,1)S(1)} %fusion.21), kind=kOutput, calls=%fused_computation.24 | convolution fusion | flops 1088421888 | bytes 9175072 | tf_op jit(solution)/shard_map/phj,jhd->phd/dot_general | solution.py:40
  31.9 56.9 %while.12 = (s32[]{:T(128)}, bf16[128,512]{1,0:T(8,128)(2,1)S(1)}, f32[128,1024]{0,1:T(8,128)}, bf16[512,1024]{1,0:T(8,128)(2,1)S(1)}, bf16[2048,1024]{1,0:T(8,1...) while((s32[]{:T(128)}, bf16[128,512]{1,0:T(8,128)(2,1)S(1)}, ...), condition=%wide.region_1.2_spmd, body=%wide.region_0.1_spmd.sunk | while | flops 1222901760 | bytes 15073477 | solution.py:83
  31.9 3.0 %collective-permute-start = (bf16[128,512]{1,0:T(8,128)(2,1)S(1)}, bf16[128,512]{1,0:T(8,128)(2,1)S(1)}, u32[]{:S(2)}, u32[]{:S(2)}) collective-permute-start(bf16[128,512]{1,0:T(8,128)(2,1)S(1)} %get-tuple-element.122), channel_id=1, source_target_pairs={{0,4},{4,8},{8,12},{12,0},{1,5},{5,9},{9,13},{13,1},{2,6},{6,10},{... | collective-permute-start | bytes 393224 | tf_op jit(solution)/shard_map/while/body/eval_jaxpr/ppermute | solution.py:15
  34.9 1.6 %collective-permute-start.1 = (f32[128,1024]{0,1:T(8,128)}, f32[128,1024]{0,1:T(8,128)S(1)}, u32[]{:S(2)}, u32[]{:S(2)}) collective-permute-start(f32[128,1024]{0,1:T(8,128)} %get-tuple-element.123), channel_id=1, source_target_pairs={{0,4},{4,8},{8,12},{12,0},{1,5},{5,9},{9,13},{13,1},{2,6},{6,10},{... | collective-permute-start | bytes 1572872 | tf_op jit(solution)/shard_map/while/body/eval_jaxpr/ppermute | solution.py:15
  36.5 4.8 %collective-permute-done = bf16[128,512]{1,0:T(8,128)(2,1)S(1)} collective-permute-done((bf16[128,512]{1,0:T(8,128)(2,1)S(1)}, bf16[128,512]{1,0:T(8,128)(2,1)S(1)}, u32[]{:S(2)}, u32[]{:S(2)}) %collective-permute-start) | collective-permute-done | bytes 131104 | tf_op jit(solution)/shard_map/while/body/eval_jaxpr/ppermute | solution.py:15
  41.6 6.3 %fusion.74 = f32[8,128,128]{1,2,0:T(8,128)S(1)} fusion(bf16[2048,8,128]{0,2,1:T(8,128)(2,1)} %bitcast.122, f32[8]{0:T(128)S(1)} %bitcast.132, bf16[16,8,8,128]{3,2,1,0:T(8,128)(2,1)S(1)} %fusion.73, bf16[2048,1024]{1,0:T(8,128)(2,1)} %get-tuple-element.133), kind=kOutput, calls=%fused_computation.8.clone.1 | convolution fusion | flops 1088421888 | bytes 9175072 | tf_op jit(solution)/shard_map/while/body/eval_jaxpr/phj,jhd->phd/dot_general | solution.py:40
  47.9 3.8 %collective-permute-done.1 = f32[128,1024]{0,1:T(8,128)S(1)} collective-permute-done((f32[128,1024]{0,1:T(8,128)}, f32[128,1024]{0,1:T(8,128)S(1)}, u32[]{:S(2)}, u32[]{:S(2)}) %collective-permute-start.1) | collective-permute-done | bytes 524320 | tf_op jit(solution)/shard_map/while/body/eval_jaxpr/ppermute | solution.py:15
  52.6 1.3 collective-permute-start.1
  53.8 6.9 %collective-permute-done = bf16[128,512]{1,0:T(8,128)(2,1)S(1)} collective-permute-done((bf16[128,512]{1,0:T(8,128)(2,1)S(1)}, bf16[128,512]{1,0:T(8,128)(2,1)S(1)}, u32[]{:S(2)}, u32[]{:S(2)}) %collective-permute-start) | collective-permute-done | bytes 131104 | tf_op jit(solution)/shard_map/while/body/eval_jaxpr/ppermute | solution.py:15
  61.1 6.3 %fusion.74 = f32[8,128,128]{1,2,0:T(8,128)S(1)} fusion(bf16[2048,8,128]{0,2,1:T(8,128)(2,1)} %bitcast.122, f32[8]{0:T(128)S(1)} %bitcast.132, bf16[16,8,8,128]{3,2,1,0:T(8,128)(2,1)S(1)} %fusion.73, bf16[2048,1024]{1,0:T(8,128)(2,1)} %get-tuple-element.133), kind=kOutput, calls=%fused_computation.8.clone.1 | convolution fusion | flops 1088421888 | bytes 9175072 | tf_op jit(solution)/shard_map/while/body/eval_jaxpr/phj,jhd->phd/dot_general | solution.py:40
  67.4 2.9 %collective-permute-done.1 = f32[128,1024]{0,1:T(8,128)S(1)} collective-permute-done((f32[128,1024]{0,1:T(8,128)}, f32[128,1024]{0,1:T(8,128)S(1)}, u32[]{:S(2)}, u32[]{:S(2)}) %collective-permute-start.1) | collective-permute-done | bytes 524320 | tf_op jit(solution)/shard_map/while/body/eval_jaxpr/ppermute | solution.py:15
  71.2 8.2 %collective-permute-done = bf16[128,512]{1,0:T(8,128)(2,1)S(1)} collective-permute-done((bf16[128,512]{1,0:T(8,128)(2,1)S(1)}, bf16[128,512]{1,0:T(8,128)(2,1)S(1)}, u32[]{:S(2)}, u32[]{:S(2)}) %collective-permute-start) | collective-permute-done | bytes 131104 | tf_op jit(solution)/shard_map/while/body/eval_jaxpr/ppermute | solution.py:15
  79.7 6.3 %fusion.74 = f32[8,128,128]{1,2,0:T(8,128)S(1)} fusion(bf16[2048,8,128]{0,2,1:T(8,128)(2,1)} %bitcast.122, f32[8]{0:T(128)S(1)} %bitcast.132, bf16[16,8,8,128]{3,2,1,0:T(8,128)(2,1)S(1)} %fusion.73, bf16[2048,1024]{1,0:T(8,128)(2,1)} %get-tuple-element.133), kind=kOutput, calls=%fused_computation.8.clone.1 | convolution fusion | flops 1088421888 | bytes 9175072 | tf_op jit(solution)/shard_map/while/body/eval_jaxpr/phj,jhd->phd/dot_general | solution.py:40
  86.0 1.9 %collective-permute-done.1 = f32[128,1024]{0,1:T(8,128)S(1)} collective-permute-done((f32[128,1024]{0,1:T(8,128)}, f32[128,1024]{0,1:T(8,128)S(1)}, u32[]{:S(2)}, u32[]{:S(2)}) %collective-permute-start.1) | collective-permute-done | bytes 524320 | tf_op jit(solution)/shard_map/while/body/eval_jaxpr/ppermute | solution.py:15
  88.8 2.2 %fusion.37 = f32[128,512]{1,0:T(8,128)S(1)} fusion(f32[128,1024]{0,1:T(8,128)} %get-tuple-element.39, bf16[1024,512]{1,0:T(8,128)(2,1)} %param.22), kind=kOutput, calls=%fused_computation.50 | convolution fusion | flops 805306368 | bytes 1835008 | tf_op jit(solution)/shard_map/dot_general | solution.py:86
  91.0 9.6 %all_to_all.10 = f32[4,32,512]{2,1,0:T(8,128)S(1)} all-to-all(f32[4,32,512]{2,1,0:T(8,128)S(1)} %bitcast.126), channel_id=1, replica_groups=mesh['groups'=2,'obs'=4,'hid'=2,'rep'=2] {'obs'}, dimensions={0} | all-to-all | bytes 524288 | tf_op jit(solution)/shard_map/all_to_all | solution.py:90
  100.7 3.4 %all-to-all-start = ((f32[4,32,512]{2,1,0:T(8,128)}), f32[4,32,512]{2,1,0:T(8,128)S(1)}, u32[]{:S(2)}, u32[]{:S(2)}) async-start(f32[4,32,512]{2,1,0:T(8,128)} %bitcast.127), calls=%async_computation | async-start | bytes 524288 | tf_op jit(solution)/shard_map/all_to_all | solution.py:69
  105.4 5.4 %all-to-all-done = f32[4,32,512]{2,1,0:T(8,128)S(1)} async-done(((f32[4,32,512]{2,1,0:T(8,128)}), f32[4,32,512]{2,1,0:T(8,128)S(1)}, u32[]{:S(2)}, u32[]{:S(2)}) %all-to-all-start) | async-done | bytes 262176 | tf_op jit(solution)/shard_map/all_to_all | solution.py:69
  110.8 1.7 %fusion.24 = f32[1,128,512]{2,1,0:T(8,128)S(1)} fusion(f32[1,128,512]{2,1,0:T(8,128)S(1)} %copy.60, s32[]{:T(128)S(6)} %select_n.2, bf16[1024,512]{1,0:T(8,128)(2,1)S(1)} %copy-done.7, bf16[512,1024]{1,0:T(8,128)(2,1)} %param.23, f32[1024]{0:T(1024)S(1)} %bitcast.130, f32[128,512]{1,0:T(8,128)S(1)} %bitcast.129, f32[128,512]{1,0:T(8,128)S(1)} %bitcast.125), kind=kOutput, calls=%fused_computation.31 | convolution fusion | flops 134676480 | bytes 2429952 | tf_op jit(solution)/shard_map/dot_general | solution.py:100
  113.4 16.1 %all-gather.2.cloned.1.call-done = f32[4,128,512]{2,1,0:T(8,128)} async-done(((f32[1,128,512]{2,1,0:T(8,128)}), f32[4,128,512]{2,1,0:T(8,128)}) %all-gather.2.cloned.1.call-update) | async-done | bytes 1048592 | tf_op jit(solution)/shard_map/all_gather | solution.py:107
  129.4 1.3 reduce_sum.9
  (44 shorter events, 7.3 us)
Async XLA Ops:
  7.2 1.2 copy-start
  8.4 4.4 %copy-start.5 = (bf16[256,1024]{1,0:T(8,128)(2,1)S(1)}, bf16[256,1024]{1,0:T(8,128)(2,1)}, u32[]{:S(2)}) copy-start(bf16[256,1024]{1,0:T(8,128)(2,1)} %param.19) | copy-start | bytes 1572868
  12.8 3.3 %copy-start.3 = (f32[1,128,512]{2,1,0:T(8,128)S(1)}, f32[1,128,512]{2,1,0:T(8,128)}, u32[]{:S(2)}) copy-start(f32[1,128,512]{2,1,0:T(8,128)} %param.14) | copy-start | bytes 786436
  16.1 6.5 %copy-start.8 = (bf16[256,8]{0,1:T(8,128)(2,1)S(1)}, bf16[256,8]{0,1:T(8,128)(2,1)}, u32[]{:S(2)}) copy-start(bf16[256,8]{0,1:T(8,128)(2,1)} %param.21) | copy-start | bytes 12292
  16.1 6.6 %copy-start.1 = (bf16[512,1024]{1,0:T(8,128)(2,1)S(1)}, bf16[512,1024]{1,0:T(8,128)(2,1)}, u32[]{:S(2)}) copy-start(bf16[512,1024]{1,0:T(8,128)(2,1)} %param.18) | copy-start | bytes 3145732
  31.9 9.4 %collective-permute-start = (bf16[128,512]{1,0:T(8,128)(2,1)S(1)}, bf16[128,512]{1,0:T(8,128)(2,1)S(1)}, u32[]{:S(2)}, u32[]{:S(2)}) collective-permute-start(bf16[128,512]{1,0:T(8,128)(2,1)S(1)} %get-tuple-element.122), channel_id=1, source_target_pairs={{0,4},{4,8},{8,12},{12,0},{1,5},{5,9},{9,13},{13,1},{2,6},{6,10},{... | collective-permute-start | bytes 393224 | tf_op jit(solution)/shard_map/while/body/eval_jaxpr/ppermute | solution.py:15
  34.9 16.8 %collective-permute-start.1 = (f32[128,1024]{0,1:T(8,128)}, f32[128,1024]{0,1:T(8,128)S(1)}, u32[]{:S(2)}, u32[]{:S(2)}) collective-permute-start(f32[128,1024]{0,1:T(8,128)} %get-tuple-element.123), channel_id=1, source_target_pairs={{0,4},{4,8},{8,12},{12,0},{1,5},{5,9},{9,13},{13,1},{2,6},{6,10},{... | collective-permute-start | bytes 1572872 | tf_op jit(solution)/shard_map/while/body/eval_jaxpr/ppermute | solution.py:15
  52.5 8.2 %collective-permute-start = (bf16[128,512]{1,0:T(8,128)(2,1)S(1)}, bf16[128,512]{1,0:T(8,128)(2,1)S(1)}, u32[]{:S(2)}, u32[]{:S(2)}) collective-permute-start(bf16[128,512]{1,0:T(8,128)(2,1)S(1)} %get-tuple-element.122), channel_id=1, source_target_pairs={{0,4},{4,8},{8,12},{12,0},{1,5},{5,9},{9,13},{13,1},{2,6},{6,10},{... | collective-permute-start | bytes 393224 | tf_op jit(solution)/shard_map/while/body/eval_jaxpr/ppermute | solution.py:15
  52.6 17.7 %collective-permute-start.1 = (f32[128,1024]{0,1:T(8,128)}, f32[128,1024]{0,1:T(8,128)S(1)}, u32[]{:S(2)}, u32[]{:S(2)}) collective-permute-start(f32[128,1024]{0,1:T(8,128)} %get-tuple-element.123), channel_id=1, source_target_pairs={{0,4},{4,8},{8,12},{12,0},{1,5},{5,9},{9,13},{13,1},{2,6},{6,10},{... | collective-permute-start | bytes 1572872 | tf_op jit(solution)/shard_map/while/body/eval_jaxpr/ppermute | solution.py:15
  71.1 8.2 %collective-permute-start = (bf16[128,512]{1,0:T(8,128)(2,1)S(1)}, bf16[128,512]{1,0:T(8,128)(2,1)S(1)}, u32[]{:S(2)}, u32[]{:S(2)}) collective-permute-start(bf16[128,512]{1,0:T(8,128)(2,1)S(1)} %get-tuple-element.122), channel_id=1, source_target_pairs={{0,4},{4,8},{8,12},{12,0},{1,5},{5,9},{9,13},{13,1},{2,6},{6,10},{... | collective-permute-start | bytes 393224 | tf_op jit(solution)/shard_map/while/body/eval_jaxpr/ppermute | solution.py:15
  71.2 16.8 %collective-permute-start.1 = (f32[128,1024]{0,1:T(8,128)}, f32[128,1024]{0,1:T(8,128)S(1)}, u32[]{:S(2)}, u32[]{:S(2)}) collective-permute-start(f32[128,1024]{0,1:T(8,128)} %get-tuple-element.123), channel_id=1, source_target_pairs={{0,4},{4,8},{8,12},{12,0},{1,5},{5,9},{9,13},{13,1},{2,6},{6,10},{... | collective-permute-start | bytes 1572872 | tf_op jit(solution)/shard_map/while/body/eval_jaxpr/ppermute | solution.py:15
  88.8 22.0 %copy-start.7 = (bf16[1024,512]{1,0:T(8,128)(2,1)S(1)}, bf16[1024,512]{1,0:T(8,128)(2,1)}, u32[]{:S(2)}) copy-start(bf16[1024,512]{1,0:T(8,128)(2,1)} %param.25) | copy-start | bytes 3145732
  91.0 39.8 %copy-start.6 = (f32[4,32,512]{2,1,0:T(8,128)S(1)}, f32[4,32,512]{2,1,0:T(8,128)}, u32[]{:S(2)}) copy-start(f32[4,32,512]{2,1,0:T(8,128)} %param.17) | copy-start | bytes 786436
  100.7 10.2 %all-to-all-start = ((f32[4,32,512]{2,1,0:T(8,128)}), f32[4,32,512]{2,1,0:T(8,128)S(1)}, u32[]{:S(2)}, u32[]{:S(2)}) async-start(f32[4,32,512]{2,1,0:T(8,128)} %bitcast.127), calls=%async_computation | async-start | bytes 524288 | tf_op jit(solution)/shard_map/all_to_all | solution.py:69
  104.1 25.4 %all-gather.2.cloned.1.call-start = ((), (), s32[]{:S(2)}) async-start(), calls=%async_computation.2 | async-start | bytes 1310720 | tf_op jit(solution)/shard_map/all_gather | solution.py:107
  112.5 0.7 copy-start.4
  130.8 0.8 copy-start.2
Sparse Core Ops, SparseCore 0:
  113.4 15.9 all-gather.1
